TPU v7x, 256 devices: a whole 4x4x8 slice. The times are simulated.
256 devices in a mesh: gx: 16 (over z, core), gy: 16 (over y, x).
Axes of the slice: x: 4, y: 4, z: 8, core: 2. Of those that a mesh axis runs over, the one named last changes fastest.
Arguments:
- populations: float32 [19, 8, 128, 2048], P(None, None, 'gy', 'gx'), may hold values from 0.49 to 22.2, as said below
- concentrations: float32 [3, 8, 128, 2048], P(None, None, 'gy', 'gx'), may hold values from 0.5 to 2
- potential: float32 [8, 128, 2048], P(None, 'gy', 'gx'), may hold values from -5 to 5
- solid_mask: int32 [8, 128, 2048], P(None, 'gy', 'gx'), may hold values 0 or 1
- surface_sign: int32 [8, 128, 2048], P(None, 'gy', 'gx'), may hold values from -1 to 1
Outputs:
- populations_new: float32 [19, 8, 128, 2048], P(None, None, 'gy', 'gx')
- concentrations_new: float32 [3, 8, 128, 2048], P(None, None, 'gy', 'gx')
- potential_new: float32 [8, 128, 2048], P(None, 'gy', 'gx')
Inputs may be any that keep to these rules, and one draw needn't show every extreme that they name: `populations`: every entry is positive, near 36 times the weight of its velocity times a density of order one. `solid_mask`: 1 marks a solid cell, 0 a fluid one. `surface_sign`: read only at solid cells.
All inputs are finite; a program needn't handle non-finite values. No bound on the sum of `solid_mask` on one device may be relied on, other than what follows from the above.
Results may differ from a plain program's by a relative error of at most 0.0018.
Values sent between devices are 32-bit elements; how exact they have to be, the bound alone decides.
No kernel may reach another device: no remote copies, remote signals or barrier semaphores. Data moves between devices by JAX's collectives and lax.ppermute only.
A program may use at most 64 MiB of HBM per device.

v0:
```python
import jax
import jax.numpy as jnp
import numpy as np
from jax import lax
from jax.sharding import PartitionSpec as P

STEPS = 4
CYCLES = 2
SSTEP = 4
lattice_velocity = (
    (0, 0, 0),
    (0, 0, 1),
    (0, 0, -1),
    (0, 1, 0),
    (0, -1, 0),
    (1, 0, 0),
    (-1, 0, 0),
    (0, 1, 1),
    (0, -1, -1),
    (0, 1, -1),
    (0, -1, 1),
    (1, 0, 1),
    (-1, 0, -1),
    (1, 0, -1),
    (-1, 0, 1),
    (1, 1, 0),
    (-1, -1, 0),
    (1, -1, 0),
    (-1, 1, 0),
)
opposite = (0, 2, 1, 4, 3, 6, 5, 8, 7, 10, 9, 12, 11, 14, 13, 16, 15, 18, 17)
lattice_weight = (1.0 / 3.0,) + (1.0 / 18.0,) * 6 + (1.0 / 36.0,) * 12
moving = (1, 2, 3, 4, 7, 8, 9, 10, 11, 12, 13, 14, 15, 16, 17, 18)
relax_time = 1.25
force_scale = 0.05
valences = (1.0, -1.0, 2.0)
diffusivity = (0.05, 0.07, 0.03)
diag_coef = 6.0001
surface_scale = 2.0


def padded_2(block, sides, width):
    for axis, dim in sides:
        count = lax.axis_size(axis)
        forward = [(i, i + 1) for i in range(count - 1)]
        forward.append((count - 1, 0))
        backward = [(target, source) for source, target in forward]
        low = lax.ppermute(
            lax.slice_in_dim(block, block.shape[dim] - width, None, axis=dim), axis, forward
        )
        high = lax.ppermute(lax.slice_in_dim(block, 0, width, axis=dim), axis, backward)
        block = jnp.concatenate([low, block, high], axis=dim)
    return block


def lattice_dot(direction, vector):
    running = None
    for axis_id in range(3):
        if direction[axis_id] != 0:
            addend = vector[axis_id] if direction[axis_id] > 0 else -vector[axis_id]
            running = addend if running is None else running + addend
    return running


def ion_charge(concentration):
    return (
        valences[0] * concentration[0]
        + valences[1] * concentration[1]
        + valences[2] * concentration[2]
    )


def collide_cells(fields, concentration, fluid_mask, efield):
    density = fields[0]
    for member in range(1, 19):
        density = density + fields[member]
    momentum = []
    for axis_id in range(3):
        running = None
        for member in range(19):
            sign_val = lattice_velocity[member][axis_id]
            if sign_val != 0:
                addend = fields[member] if sign_val > 0 else -fields[member]
                running = addend if running is None else running + addend
        momentum.append(running)
    charge = fluid_mask * ion_charge(concentration)
    forcing = [force_scale * charge * efield[axis_id] for axis_id in range(3)]
    velocity = [(momentum[axis_id] + 0.5 * forcing[axis_id]) / density for axis_id in range(3)]
    speed_sq = velocity[0] * velocity[0] + velocity[1] * velocity[1] + velocity[2] * velocity[2]
    work_rate = velocity[0] * forcing[0] + velocity[1] * forcing[1] + velocity[2] * forcing[2]
    relaxed = []
    for member in range(19):
        weight = lattice_weight[member]
        if member == 0:
            projected = jnp.zeros_like(density)
            along_force = jnp.zeros_like(density)
        else:
            projected = lattice_dot(lattice_velocity[member], velocity)
            along_force = lattice_dot(lattice_velocity[member], forcing)
        balance = (
            weight
            * density
            * (1.0 + 3.0 * projected + 4.5 * projected * projected - 1.5 * speed_sq)
        )
        source = weight * (3.0 * (along_force - work_rate) + 9.0 * projected * along_force)
        relaxed.append(
            fields[member]
            - (fields[member] - balance) / relax_time
            + (1.0 - 0.5 / relax_time) * source
        )
    return (relaxed, velocity)


def face_flux(low, high, pot_low, pot_high, vel_low, vel_high, opened):
    rates = jnp.array(diffusivity, jnp.float32).reshape(3, 1, 1, 1)
    drift = jnp.array(valences, jnp.float32).reshape(3, 1, 1, 1) * rates
    middle = 0.5 * (low + high)
    return opened * (
        -rates * (high - low)
        - drift * middle * (pot_high - pot_low)
        + 0.5 * (vel_low + vel_high) * middle
    )


def ion_step(concentration, velocity, potential, fluid_mask, ion_pad, pot_rim, fluid_rim):
    fluxes = face_flux(
        concentration,
        jnp.roll(concentration, -1, 1),
        potential,
        jnp.roll(potential, -1, 0),
        velocity[0],
        jnp.roll(velocity[0], -1, 0),
        fluid_mask * jnp.roll(fluid_mask, -1, 0),
    )
    running = fluxes - jnp.roll(fluxes, 1, 1)
    conc_in = ion_pad[:3, :, :, 1:-1]
    pot_in = pot_rim[:, :, 1:-1]
    vel_in = ion_pad[3, :, :, 1:-1]
    open_in = fluid_rim[:, :, 1:-1]
    fluxes = face_flux(
        conc_in[:, :, :-1],
        conc_in[:, :, 1:],
        pot_in[:, :-1],
        pot_in[:, 1:],
        vel_in[:, :-1],
        vel_in[:, 1:],
        open_in[:, :-1] * open_in[:, 1:],
    )
    running = running + (fluxes[:, :, 1:] - fluxes[:, :, :-1])
    conc_in = ion_pad[:3, :, 1:-1, :]
    pot_in = pot_rim[:, 1:-1, :]
    vel_in = ion_pad[4, :, 1:-1, :]
    open_in = fluid_rim[:, 1:-1, :]
    fluxes = face_flux(
        conc_in[..., :-1],
        conc_in[..., 1:],
        pot_in[..., :-1],
        pot_in[..., 1:],
        vel_in[..., :-1],
        vel_in[..., 1:],
        open_in[..., :-1] * open_in[..., 1:],
    )
    running = running + (fluxes[..., 1:] - fluxes[..., :-1])
    return concentration - running


def neighbor_sum(padded):
    core = padded[:, :, 1:-1, 1:-1]
    return (
        jnp.roll(core, -1, 1)
        + jnp.roll(core, 1, 1)
        + (padded[:, :, 2:, 1:-1] + padded[:, :, :-2, 1:-1])
        + (padded[:, :, 1:-1, 2:] + padded[:, :, 1:-1, :-2])
    )


def next_level(summed, previous):
    if previous is None:
        return -summed / 6.0
    return -summed / 3.0 - previous


def shift_table():
    order_m = 2 * SSTEP + 1
    coeffs = np.zeros((order_m, order_m), np.float32)
    for block_start in (0, SSTEP + 1):
        block_depth = SSTEP if block_start == 0 else SSTEP - 1
        for column in range(block_depth):
            coeffs[block_start + column, block_start + column] = diag_coef
            coeffs[block_start + column + 1, block_start + column] = 6.0 if column == 0 else 3.0
            if column > 0:
                coeffs[block_start + column - 1, block_start + column] = 3.0
    return coeffs


def krylov_steps(gram_matrix):
    order_m = 2 * SSTEP + 1
    highest = lax.Precision.HIGHEST
    coeffs = jnp.asarray(shift_table(), jnp.float32)
    search_co = jnp.zeros((order_m,), jnp.float32).at[0].set(1.0)
    resid_co = jnp.zeros((order_m,), jnp.float32).at[SSTEP + 1].set(1.0)
    sol_co = jnp.zeros((order_m,), jnp.float32)
    residual_sq = jnp.dot(
        resid_co, jnp.dot(gram_matrix, resid_co, precision=highest), precision=highest
    )
    for inner_id in range(SSTEP):
        image_co = jnp.dot(coeffs, search_co, precision=highest)
        step_len = residual_sq / jnp.dot(
            search_co, jnp.dot(gram_matrix, image_co, precision=highest), precision=highest
        )
        sol_co = sol_co + step_len * search_co
        resid_co = resid_co - step_len * image_co
        fresh_sq = jnp.dot(
            resid_co, jnp.dot(gram_matrix, resid_co, precision=highest), precision=highest
        )
        search_co = resid_co + fresh_sq / residual_sq * search_co
        residual_sq = fresh_sq
    return (sol_co, resid_co, search_co)


def local(populations, concentrations, potential, solid_mask, surface_sign):
    highest = lax.Precision.HIGHEST
    fluid_mask = 1.0 - solid_mask.astype(jnp.float32)
    rows_y = potential.shape[1]
    cols_x = potential.shape[2]
    rims = padded_2(jnp.stack([potential, fluid_mask]), (("gx", 3), ("gy", 2)), 1)
    pot_rim = rims[0]
    fluid_rim = rims[1]
    efield = [
        (jnp.roll(potential, 1, 0) - jnp.roll(potential, -1, 0)) * 0.5,
        (pot_rim[:, :-2, 1:-1] - pot_rim[:, 2:, 1:-1]) * 0.5,
        (pot_rim[:, 1:-1, :-2] - pot_rim[:, 1:-1, 2:]) * 0.5,
    ]
    source_open = []
    for member in range(19):
        offset = lattice_velocity[member]
        window = fluid_rim[
            :, 1 - offset[1] : 1 - offset[1] + rows_y, 1 - offset[2] : 1 - offset[2] + cols_x
        ]
        source_open.append(jnp.roll(window, offset[0], 0))
    fields = [populations[member] for member in range(19)]
    concentration = concentrations
    for time_step in range(STEPS):
        relaxed, velocity = collide_cells(fields, concentration, fluid_mask, efield)
        stacked = jnp.concatenate(
            [
                jnp.stack([relaxed[member] for member in moving]),
                concentration,
                jnp.stack([velocity[1], velocity[2]]),
            ]
        )
        lattice_pad = padded_2(stacked, (("gx", 3), ("gy", 2)), 1)
        ion_pad = lattice_pad[len(moving) :]
        arrived = []
        for member in range(19):
            offset = lattice_velocity[member]
            if member in moving:
                slot_id = moving.index(member)
                piece = lattice_pad[
                    slot_id,
                    :,
                    1 - offset[1] : 1 - offset[1] + rows_y,
                    1 - offset[2] : 1 - offset[2] + cols_x,
                ]
            else:
                piece = relaxed[member]
            arrived.append(jnp.roll(piece, offset[0], 0))
        updated = [
            jnp.where(
                fluid_mask > 0.5,
                jnp.where(source_open[member] > 0.5, arrived[member], relaxed[opposite[member]]),
                fields[member],
            )
            for member in range(19)
        ]
        concentration = ion_step(
            concentration, velocity, potential, fluid_mask, ion_pad, pot_rim, fluid_rim
        )
        fields = updated
    target = fluid_mask * ion_charge(concentration) + surface_scale * surface_sign.astype(
        jnp.float32
    ) * (1.0 - fluid_mask)
    solution = potential
    start_pad = padded_2(solution[None], (("gx", 3), ("gy", 2)), 1)
    residual = target - (diag_coef * solution - neighbor_sum(start_pad)[0])
    search = residual
    for cycle_id in range(CYCLES):
        p_levels = [search]
        r_levels = [residual]
        previous = None
        current = jnp.stack([search, residual])
        for level_id in range(SSTEP):
            if level_id == SSTEP - 1:
                current = current[:1]
            padded = padded_2(current, (("gx", 3), ("gy", 2)), 1)
            following = next_level(
                neighbor_sum(padded), None if level_id == 0 else previous[: current.shape[0]]
            )
            previous = current
            current = following
            p_levels.append(current[0])
            if current.shape[0] > 1:
                r_levels.append(current[1])
        basis = jnp.stack(p_levels + r_levels)
        local_gram = jnp.einsum("aijk,bijk->ab", basis, basis, precision=highest)
        gram_matrix = lax.psum(local_gram, ("gx", "gy"))
        sol_co, resid_co, search_co = krylov_steps(gram_matrix)
        solution = solution + jnp.tensordot(sol_co, basis, axes=1, precision=highest)
        residual = jnp.tensordot(resid_co, basis, axes=1, precision=highest)
        search = jnp.tensordot(search_co, basis, axes=1, precision=highest)
    return (jnp.stack(fields), concentration, solution)


def solution(mesh):
    placed = (
        P(None, None, "gy", "gx"),
        P(None, None, "gy", "gx"),
        P(None, "gy", "gx"),
        P(None, "gy", "gx"),
        P(None, "gy", "gx"),
    )
    return jax.shard_map(
        local,
        mesh=mesh,
        in_specs=placed,
        out_specs=(P(None, None, "gy", "gx"), P(None, None, "gy", "gx"), P(None, "gy", "gx")),
        check_vma=False,
    )
```

profile of v0, /device:TPU:1, one launch (start us, length us, event | category | flops | bytes accessed | tf_op | source)
XLA Modules:
  0.0 479.0 jit_solution(2040877553520355775)
XLA Ops:
  11.4 3.8 collective-permute-start.3
  32.1 3.3 collective-permute-start.5
  43.5 5.4 %collective-permute-start.7 = (f32[21,8,1,130]{3,2,1,0:T(1,128)S(1)}, f32[21,8,1,130]{3,2,1,0:T(1,128)S(1)}, u32[]{:S(2)}, u32[]{:S(2)}) collective-permute-start(f32[21,8,1,130]{3,2,1,0:T(1,128)S(1)} %get-tuple-element.347), channel_id=1, source_target_pairs={{1,0},{2,1},{3,2},{4,3},{5,4},{6,5},{7,6},{8,7},{9,8},{10,9},{11,1... | collective-permute-start | bytes 262088 | tf_op jit(solution)/shard_map/ppermute | solution.py:51
  79.4 5.8 %collective-permute-start.11 = (f32[21,8,1,130]{3,2,1,0:T(1,128)S(1)}, f32[21,8,1,130]{3,2,1,0:T(1,128)S(1)}, u32[]{:S(2)}, u32[]{:S(2)}) collective-permute-start(f32[21,8,1,130]{3,2,1,0:T(1,128)S(1)} %get-tuple-element.341), channel_id=1, source_target_pairs={{1,0},{2,1},{3,2},{4,3},{5,4},{6,5},{7,6},{8,7},{9,8},{10,9},{11,1... | collective-permute-start | bytes 262088 | tf_op jit(solution)/shard_map/ppermute | solution.py:51
  115.1 5.6 %collective-permute-start.15 = (f32[21,8,1,130]{3,2,1,0:T(1,128)S(1)}, f32[21,8,1,130]{3,2,1,0:T(1,128)S(1)}, u32[]{:S(2)}, u32[]{:S(2)}) collective-permute-start(f32[21,8,1,130]{3,2,1,0:T(1,128)S(1)} %get-tuple-element.335), channel_id=1, source_target_pairs={{1,0},{2,1},{3,2},{4,3},{5,4},{6,5},{7,6},{8,7},{9,8},{10,9},{11,1... | collective-permute-start | bytes 262088 | tf_op jit(solution)/shard_map/ppermute | solution.py:51
  141.5 3.2 collective-permute-start.17
  146.2 5.1 %collective-permute-start.22 = (f32[1,8,1,130]{3,2,1,0:T(1,128)}, f32[1,8,1,130]{3,2,1,0:T(1,128)}, u32[]{:S(2)}, u32[]{:S(2)}) collective-permute-start(f32[1,8,1,130]{3,2,1,0:T(1,128)} %get-tuple-element.428), channel_id=1, source_target_pairs={{1,0},{2,1},{3,2},{4,3},{5,4},{6,5},{7,6},{8,7},{9,8},{10,9},{11,1... | collective-permute-start | bytes 12488 | tf_op jit(solution)/shard_map/ppermute | solution.py:51
  156.5 4.8 %collective-permute-start.19 = (f32[21,8,1,130]{3,2,1,0:T(1,128)S(1)}, f32[21,8,1,130]{3,2,1,0:T(1,128)S(1)}, u32[]{:S(2)}, u32[]{:S(2)}) collective-permute-start(f32[21,8,1,130]{3,2,1,0:T(1,128)S(1)} %get-tuple-element.328), channel_id=1, source_target_pairs={{1,0},{2,1},{3,2},{4,3},{5,4},{6,5},{7,6},{8,7},{9,8},{10,9},{11,1... | collective-permute-start | bytes 262088 | tf_op jit(solution)/shard_map/ppermute | solution.py:51
  170.8 3.6 collective-permute-start.25
  184.3 5.2 %collective-permute-start.26 = (f32[2,8,1,130]{3,0,2,1:T(2,128)S(1)}, f32[2,8,1,130]{3,0,2,1:T(2,128)S(1)}, u32[]{:S(2)}, u32[]{:S(2)}) collective-permute-start(f32[2,8,1,130]{3,0,2,1:T(2,128)S(1)} %get-tuple-element.402), channel_id=1, source_target_pairs={{1,0},{2,1},{3,2},{4,3},{5,4},{6,5},{7,6},{8,7},{9,8},{10,9},{11,1... | collective-permute-start | bytes 24968 | tf_op jit(solution)/shard_map/ppermute | solution.py:51
  190.4 5.0 %collective-permute-done.27 = f32[2,8,1,130]{3,0,2,1:T(2,128)S(1)} collective-permute-done((f32[2,8,1,130]{3,0,2,1:T(2,128)S(1)}, f32[2,8,1,130]{3,0,2,1:T(2,128)S(1)}, u32[]{:S(2)}, u32[]{:S(2)}) %collective-permute-start.27) | collective-permute-done | bytes 8352 | tf_op jit(solution)/shard_map/ppermute | solution.py:48
  196.2 4.4 collective-permute-start.29
  204.5 3.1 collective-permute-done.31
  208.2 5.1 %collective-permute-start.33 = (f32[2,8,8,1]{3,0,2,1:T(2,128)S(1)}, f32[2,8,8,1]{3,0,2,1:T(2,128)S(1)}, u32[]{:S(2)}, u32[]{:S(2)}) collective-permute-start(f32[2,8,8,1]{3,0,2,1:T(2,128)S(1)} %get-tuple-element.487), channel_id=1, source_target_pairs={{16,0},{32,16},{48,32},{64,48},{80,64},{96,80},{112,96},{128,112},... | collective-permute-start | bytes 1544 | tf_op jit(solution)/shard_map/ppermute | solution.py:51
  217.4 3.3 collective-permute-done.35
  221.3 5.1 %collective-permute-start.37 = (f32[1,8,8,1]{3,0,2,1:T(1,128)S(1)}, f32[1,8,8,1]{3,0,2,1:T(1,128)S(1)}, u32[]{:S(2)}, u32[]{:S(2)}) collective-permute-start(f32[1,8,8,1]{3,0,2,1:T(1,128)S(1)} %get-tuple-element.481), channel_id=1, source_target_pairs={{16,0},{32,16},{48,32},{64,48},{80,64},{96,80},{112,96},{128,112},... | collective-permute-start | bytes 776 | tf_op jit(solution)/shard_map/ppermute | solution.py:51
  230.3 3.1 collective-permute-done.39
  235.1 78.9 %psum.14 = f32[9,9]{1,0:T(8,128)S(1)} all-reduce(f32[9,9]{1,0:T(8,128)S(1)} %convolution_bitcast_fusion.1), channel_id=1, replica_groups=mesh['gx'=16,'gy'=16] {'gx','gy'}, use_global_device_ids=true, to_apply=%region_0.1 | all-reduce | flops 81 | bytes 648 | tf_op jit(solution)/shard_map/psum | solution.py:306
  340.5 4.5 collective-permute-done.43
  353.8 3.4 collective-permute-done.47
  366.1 3.1 collective-permute-done.51
  370.8 4.2 collective-permute-start.53
  378.9 3.1 collective-permute-done.55
  383.7 77.5 %psum.15 = f32[9,9]{1,0:T(8,128)S(1)} all-reduce(f32[9,9]{1,0:T(8,128)S(1)} %convolution_bitcast_fusion), channel_id=1, replica_groups=mesh['gx'=16,'gy'=16] {'gx','gy'}, use_global_device_ids=true, to_apply=%region_1.2 | all-reduce | flops 81 | bytes 648 | tf_op jit(solution)/shard_map/psum | solution.py:306
  (948 shorter events, 203.9 us)
Async XLA Ops:
  2.4 7.5 %collective-permute-start = (f32[2,8,8,1]{3,2,1,0:T(8,128)S(1)}, f32[2,8,8,1]{3,2,1,0:T(8,128)S(1)}, u32[]{:S(2)}, u32[]{:S(2)}) collective-permute-start(f32[2,8,8,1]{3,2,1,0:T(8,128)S(1)} %get-tuple-element.495), channel_id=1, source_target_pairs={{0,16},{16,32},{32,48},{48,64},{64,80},{80,96},{96,112},{112,128},... | collective-permute-start | bytes 1544 | tf_op jit(solution)/shard_map/ppermute | solution.py:48
  6.4 138.3 %collective-permute-start.20 = (f32[1,8,8,1]{3,2,1,0:T(8,128)}, f32[1,8,8,1]{3,2,1,0:T(8,128)}, u32[]{:S(2)}, u32[]{:S(2)}) collective-permute-start(f32[1,8,8,1]{3,2,1,0:T(8,128)} %get-tuple-element.508), channel_id=1, source_target_pairs={{0,16},{16,32},{32,48},{48,64},{64,80},{80,96},{96,112},{112,128},... | collective-permute-start | bytes 776 | tf_op jit(solution)/shard_map/ppermute | solution.py:48
  7.9 136.8 %collective-permute-start.21 = (f32[1,8,8,1]{3,2,1,0:T(8,128)}, f32[1,8,8,1]{3,2,1,0:T(8,128)}, u32[]{:S(2)}, u32[]{:S(2)}) collective-permute-start(f32[1,8,8,1]{3,2,1,0:T(8,128)} %get-tuple-element.507), channel_id=1, source_target_pairs={{16,0},{32,16},{48,32},{64,48},{80,64},{96,80},{112,96},{128,112},... | collective-permute-start | bytes 776 | tf_op jit(solution)/shard_map/ppermute | solution.py:51
  30.9 8.9 %collective-permute-start.4 = (f32[21,8,8,1]{0,2,3,1:T(8,128)S(1)}, f32[21,8,8,1]{0,2,3,1:T(8,128)S(1)}, u32[]{:S(2)}, u32[]{:S(2)}) collective-permute-start(f32[21,8,8,1]{0,2,3,1:T(8,128)S(1)} %copy.34), channel_id=1, source_target_pairs={{0,16},{16,32},{32,48},{48,64},{64,80},{80,96},{96,112},{112,128},... | collective-permute-start | bytes 16136 | tf_op jit(solution)/shard_map/ppermute | solution.py:48
  32.1 8.4 %collective-permute-start.5 = (f32[21,8,8,1]{0,2,3,1:T(8,128)S(1)}, f32[21,8,8,1]{0,2,3,1:T(8,128)}, u32[]{:S(2)}, u32[]{:S(2)}) collective-permute-start(f32[21,8,8,1]{0,2,3,1:T(8,128)S(1)} %copy.36), channel_id=1, source_target_pairs={{16,0},{32,16},{48,32},{64,48},{80,64},{96,80},{112,96},{128,112},... | collective-permute-start | bytes 16136 | tf_op jit(solution)/shard_map/ppermute | solution.py:51
  43.4 7.9 %collective-permute-start.6 = (f32[21,8,1,130]{3,2,1,0:T(1,128)S(1)}, f32[21,8,1,130]{3,2,1,0:T(1,128)S(1)}, u32[]{:S(2)}, u32[]{:S(2)}) collective-permute-start(f32[21,8,1,130]{3,2,1,0:T(1,128)S(1)} %get-tuple-element.346), channel_id=1, source_target_pairs={{0,1},{1,2},{2,3},{3,4},{4,5},{5,6},{6,7},{7,8},{8,9},{9,10},{10,1... | collective-permute-start | bytes 262088 | tf_op jit(solution)/shard_map/ppermute | solution.py:48
  43.5 7.8 %collective-permute-start.7 = (f32[21,8,1,130]{3,2,1,0:T(1,128)S(1)}, f32[21,8,1,130]{3,2,1,0:T(1,128)S(1)}, u32[]{:S(2)}, u32[]{:S(2)}) collective-permute-start(f32[21,8,1,130]{3,2,1,0:T(1,128)S(1)} %get-tuple-element.347), channel_id=1, source_target_pairs={{1,0},{2,1},{3,2},{4,3},{5,4},{6,5},{7,6},{8,7},{9,8},{10,9},{11,1... | collective-permute-start | bytes 262088 | tf_op jit(solution)/shard_map/ppermute | solution.py:51
  69.0 7.5 %collective-permute-start.8 = (f32[21,8,8,1]{0,2,3,1:T(8,128)S(1)}, f32[21,8,8,1]{0,2,3,1:T(8,128)S(1)}, u32[]{:S(2)}, u32[]{:S(2)}) collective-permute-start(f32[21,8,8,1]{0,2,3,1:T(8,128)S(1)} %copy.40), channel_id=1, source_target_pairs={{0,16},{16,32},{32,48},{48,64},{64,80},{80,96},{96,112},{112,128},... | collective-permute-start | bytes 16136 | tf_op jit(solution)/shard_map/ppermute | solution.py:48
  70.3 6.9 %collective-permute-start.9 = (f32[21,8,8,1]{0,2,3,1:T(8,128)S(1)}, f32[21,8,8,1]{0,2,3,1:T(8,128)S(1)}, u32[]{:S(2)}, u32[]{:S(2)}) collective-permute-start(f32[21,8,8,1]{0,2,3,1:T(8,128)S(1)} %copy.42), channel_id=1, source_target_pairs={{16,0},{32,16},{48,32},{64,48},{80,64},{96,80},{112,96},{128,112},... | collective-permute-start | bytes 16136 | tf_op jit(solution)/shard_map/ppermute | solution.py:51
  79.4 8.2 %collective-permute-start.10 = (f32[21,8,1,130]{3,2,1,0:T(1,128)S(1)}, f32[21,8,1,130]{3,2,1,0:T(1,128)S(1)}, u32[]{:S(2)}, u32[]{:S(2)}) collective-permute-start(f32[21,8,1,130]{3,2,1,0:T(1,128)S(1)} %get-tuple-element.340), channel_id=1, source_target_pairs={{0,1},{1,2},{2,3},{3,4},{4,5},{5,6},{6,7},{7,8},{8,9},{9,10},{10,1... | collective-permute-start | bytes 262088 | tf_op jit(solution)/shard_map/ppermute | solution.py:48
  79.4 8.2 %collective-permute-start.11 = (f32[21,8,1,130]{3,2,1,0:T(1,128)S(1)}, f32[21,8,1,130]{3,2,1,0:T(1,128)S(1)}, u32[]{:S(2)}, u32[]{:S(2)}) collective-permute-start(f32[21,8,1,130]{3,2,1,0:T(1,128)S(1)} %get-tuple-element.341), channel_id=1, source_target_pairs={{1,0},{2,1},{3,2},{4,3},{5,4},{6,5},{7,6},{8,7},{9,8},{10,9},{11,1... | collective-permute-start | bytes 262088 | tf_op jit(solution)/shard_map/ppermute | solution.py:51
  104.7 7.4 %collective-permute-start.12 = (f32[21,8,8,1]{0,2,3,1:T(8,128)S(1)}, f32[21,8,8,1]{0,2,3,1:T(8,128)S(1)}, u32[]{:S(2)}, u32[]{:S(2)}) collective-permute-start(f32[21,8,8,1]{0,2,3,1:T(8,128)S(1)} %copy.46), channel_id=1, source_target_pairs={{0,16},{16,32},{32,48},{48,64},{64,80},{80,96},{96,112},{112,128},... | collective-permute-start | bytes 16136 | tf_op jit(solution)/shard_map/ppermute | solution.py:48
  106.0 6.9 %collective-permute-start.13 = (f32[21,8,8,1]{0,2,3,1:T(8,128)S(1)}, f32[21,8,8,1]{0,2,3,1:T(8,128)S(1)}, u32[]{:S(2)}, u32[]{:S(2)}) collective-permute-start(f32[21,8,8,1]{0,2,3,1:T(8,128)S(1)} %copy.48), channel_id=1, source_target_pairs={{16,0},{32,16},{48,32},{64,48},{80,64},{96,80},{112,96},{128,112},... | collective-permute-start | bytes 16136 | tf_op jit(solution)/shard_map/ppermute | solution.py:51
  115.0 8.4 %collective-permute-start.14 = (f32[21,8,1,130]{3,2,1,0:T(1,128)S(1)}, f32[21,8,1,130]{3,2,1,0:T(1,128)S(1)}, u32[]{:S(2)}, u32[]{:S(2)}) collective-permute-start(f32[21,8,1,130]{3,2,1,0:T(1,128)S(1)} %get-tuple-element.334), channel_id=1, source_target_pairs={{0,1},{1,2},{2,3},{3,4},{4,5},{5,6},{6,7},{7,8},{8,9},{9,10},{10,1... | collective-permute-start | bytes 262088 | tf_op jit(solution)/shard_map/ppermute | solution.py:48
  115.1 8.3 %collective-permute-start.15 = (f32[21,8,1,130]{3,2,1,0:T(1,128)S(1)}, f32[21,8,1,130]{3,2,1,0:T(1,128)S(1)}, u32[]{:S(2)}, u32[]{:S(2)}) collective-permute-start(f32[21,8,1,130]{3,2,1,0:T(1,128)S(1)} %get-tuple-element.335), channel_id=1, source_target_pairs={{1,0},{2,1},{3,2},{4,3},{5,4},{6,5},{7,6},{8,7},{9,8},{10,9},{11,1... | collective-permute-start | bytes 262088 | tf_op jit(solution)/shard_map/ppermute | solution.py:51
  140.3 13.2 %collective-permute-start.16 = (f32[21,8,8,1]{0,2,3,1:T(8,128)S(1)}, f32[21,8,8,1]{0,2,3,1:T(8,128)S(1)}, u32[]{:S(2)}, u32[]{:S(2)}) collective-permute-start(f32[21,8,8,1]{0,2,3,1:T(8,128)S(1)} %copy.52), channel_id=1, source_target_pairs={{0,16},{16,32},{32,48},{48,64},{64,80},{80,96},{96,112},{112,128},... | collective-permute-start | bytes 16136 | tf_op jit(solution)/shard_map/ppermute | solution.py:48
  141.5 12.8 %collective-permute-start.17 = (f32[21,8,8,1]{0,2,3,1:T(8,128)S(1)}, f32[21,8,8,1]{0,2,3,1:T(8,128)S(1)}, u32[]{:S(2)}, u32[]{:S(2)}) collective-permute-start(f32[21,8,8,1]{0,2,3,1:T(8,128)S(1)} %copy.54), channel_id=1, source_target_pairs={{16,0},{32,16},{48,32},{64,48},{80,64},{96,80},{112,96},{128,112},... | collective-permute-start | bytes 16136 | tf_op jit(solution)/shard_map/ppermute | solution.py:51
  146.2 21.8 %collective-permute-start.22 = (f32[1,8,1,130]{3,2,1,0:T(1,128)}, f32[1,8,1,130]{3,2,1,0:T(1,128)}, u32[]{:S(2)}, u32[]{:S(2)}) collective-permute-start(f32[1,8,1,130]{3,2,1,0:T(1,128)} %get-tuple-element.428), channel_id=1, source_target_pairs={{1,0},{2,1},{3,2},{4,3},{5,4},{6,5},{7,6},{8,7},{9,8},{10,9},{11,1... | collective-permute-start | bytes 12488 | tf_op jit(solution)/shard_map/ppermute | solution.py:51
  151.4 16.7 %collective-permute-start.23 = (f32[1,8,1,130]{3,2,1,0:T(1,128)}, f32[1,8,1,130]{3,2,1,0:T(1,128)}, u32[]{:S(2)}, u32[]{:S(2)}) collective-permute-start(f32[1,8,1,130]{3,2,1,0:T(1,128)} %get-tuple-element.429), channel_id=1, source_target_pairs={{0,1},{1,2},{2,3},{3,4},{4,5},{5,6},{6,7},{7,8},{8,9},{9,10},{10,1... | collective-permute-start | bytes 12488 | tf_op jit(solution)/shard_map/ppermute | solution.py:48
  156.4 7.7 %collective-permute-start.18 = (f32[21,8,1,130]{3,2,1,0:T(1,128)S(1)}, f32[21,8,1,130]{3,2,1,0:T(1,128)S(1)}, u32[]{:S(2)}, u32[]{:S(2)}) collective-permute-start(f32[21,8,1,130]{3,2,1,0:T(1,128)S(1)} %get-tuple-element.329), channel_id=1, source_target_pairs={{0,1},{1,2},{2,3},{3,4},{4,5},{5,6},{6,7},{7,8},{8,9},{9,10},{10,1... | collective-permute-start | bytes 262088 | tf_op jit(solution)/shard_map/ppermute | solution.py:48
  156.5 7.6 %collective-permute-start.19 = (f32[21,8,1,130]{3,2,1,0:T(1,128)S(1)}, f32[21,8,1,130]{3,2,1,0:T(1,128)S(1)}, u32[]{:S(2)}, u32[]{:S(2)}) collective-permute-start(f32[21,8,1,130]{3,2,1,0:T(1,128)S(1)} %get-tuple-element.328), channel_id=1, source_target_pairs={{1,0},{2,1},{3,2},{4,3},{5,4},{6,5},{7,6},{8,7},{9,8},{10,9},{11,1... | collective-permute-start | bytes 262088 | tf_op jit(solution)/shard_map/ppermute | solution.py:51
  170.0 14.1 %collective-permute-start.24 = (f32[2,8,8,1]{3,0,2,1:T(2,128)S(1)}, f32[2,8,8,1]{3,0,2,1:T(2,128)S(1)}, u32[]{:S(2)}, u32[]{:S(2)}) collective-permute-start(f32[2,8,8,1]{3,0,2,1:T(2,128)S(1)} %get-tuple-element.502), channel_id=1, source_target_pairs={{0,16},{16,32},{32,48},{48,64},{64,80},{80,96},{96,112},{112,128},... | collective-permute-start | bytes 1544 | tf_op jit(solution)/shard_map/ppermute | solution.py:48
  170.8 13.4 %collective-permute-start.25 = (f32[2,8,8,1]{3,0,2,1:T(2,128)S(1)}, f32[2,8,8,1]{3,0,2,1:T(2,128)S(1)}, u32[]{:S(2)}, u32[]{:S(2)}) collective-permute-start(f32[2,8,8,1]{3,0,2,1:T(2,128)S(1)} %get-tuple-element.501), channel_id=1, source_target_pairs={{16,0},{32,16},{48,32},{64,48},{80,64},{96,80},{112,96},{128,112},... | collective-permute-start | bytes 1544 | tf_op jit(solution)/shard_map/ppermute | solution.py:51
  214.5 6.2 %collective-permute-start.35 = (f32[2,8,1,130]{3,0,2,1:T(2,128)S(1)}, f32[2,8,1,130]{3,0,2,1:T(2,128)S(1)}, u32[]{:S(2)}, u32[]{:S(2)}) collective-permute-start(f32[2,8,1,130]{3,0,2,1:T(2,128)S(1)} %get-tuple-element.397), channel_id=1, source_target_pairs={{0,1},{1,2},{2,3},{3,4},{4,5},{5,6},{6,7},{7,8},{8,9},{9,10},{10,1... | collective-permute-start | bytes 24968 | tf_op jit(solution)/shard_map/ppermute | solution.py:48
  (307 other events, 840.9 us)
where the time goes:
time: 488 us; the launch traced here: 479 us
  blocking collectives  156 us (32%)
  starting transfers between devices  104 us (21%)
  other arithmetic  70.3 us (14%)
  waiting for transfers between devices  55.8 us (11%)
  local copies, waits for them, and re-layouts  50.7 us (10%)
  between operations  25.1 us (5%)
  matrix products  17.1 us (4%)
    psum x2, blocking collectives, local(): gram_matrix = lax.psum(local_gram, ('gx', 'gy'))  156 us
    ppermute x28, starting transfers between devices, padded_2(): lax.ppermute(lax.slice_in_dim(block, 0, width, axis=dim), axis, backward)  80.6 us
    unnamed x81, other arithmetic  41.9 us
    ppermute x28, waiting for transfers between devices, padded_2(): lax.ppermute(lax.slice_in_dim(block, block.shape[dim] - width, None, axis...  41.5 us
    ppermute x28, starting transfers between devices, padded_2(): lax.ppermute(lax.slice_in_dim(block, block.shape[dim] - width, None, axis...  23 us
    unnamed x538, local copies, waits for them, and re-layouts  22.3 us
    ppermute x28, waiting for transfers between devices, padded_2(): lax.ppermute(lax.slice_in_dim(block, 0, width, axis=dim), axis, backward)  14.2 us
  transfers between devices with their start and end apart: 56, of which 35 were waited for; matrix products, arithmetic and copies ran while one was open for 18% of the time, Pallas kernels for 0%

commit v1 on v0

--- a/solution.py
+++ b/solution.py
@@ -3,6 +3,7 @@
 import numpy as np
 from jax import lax
 from jax.sharding import PartitionSpec as P
+from jax.lax import psum
 
 STEPS = 4
 CYCLES = 2
@@ -303,7 +304,7 @@
                 r_levels.append(current[1])
         basis = jnp.stack(p_levels + r_levels)
         local_gram = jnp.einsum("aijk,bijk->ab", basis, basis, precision=highest)
-        gram_matrix = lax.psum(local_gram, ("gx", "gy"))
+        gram_matrix = psum(psum(local_gram, axis_name="gx"), axis_name="gy")
         sol_co, resid_co, search_co = krylov_steps(gram_matrix)
         solution = solution + jnp.tensordot(sol_co, basis, axes=1, precision=highest)
         residual = jnp.tensordot(resid_co, basis, axes=1, precision=highest)

time: 488 us -> 462 us (0.947)
  the two profiles are of different devices: /device:TPU:1 before, /device:TPU:2 now
where the time goes in v1:
time: 462 us; the launch traced here: 453 us
  blocking collectives  130 us (28%)
  starting transfers between devices  99.6 us (22%)
  other arithmetic  70.3 us (15%)
  waiting for transfers between devices  61.4 us (13%)
  local copies, waits for them, and re-layouts  50.6 us (11%)
  between operations  24.4 us (5%)
  matrix products  16.6 us (4%)
    psum x4, blocking collectives, local(): gram_matrix = psum(psum(local_gram, axis_name='gx'), axis_name='gy')  130 us
    ppermute x28, starting transfers between devices, padded_2(): lax.ppermute(lax.slice_in_dim(block, 0, width, axis=dim), axis, backward)  89.9 us
    ppermute x28, waiting for transfers between devices, padded_2(): lax.ppermute(lax.slice_in_dim(block, block.shape[dim] - width, None, axis...  43.8 us
    unnamed x81, other arithmetic  41.9 us
    unnamed x538, local copies, waits for them, and re-layouts  22.3 us
    ppermute x28, waiting for transfers between devices, padded_2(): lax.ppermute(lax.slice_in_dim(block, 0, width, axis=dim), axis, backward)  17.6 us
    ppermute x28, starting transfers between devices, padded_2(): lax.ppermute(lax.slice_in_dim(block, block.shape[dim] - width, None, axis...  9.78 us
  transfers between devices with their start and end apart: 56, of which 32 were waited for; matrix products, arithmetic and copies ran while one was open for 19% of the time, Pallas kernels for 0%

profile of v1, /device:TPU:2, one launch (start us, length us, event | category | flops | bytes accessed | tf_op | source)
XLA Modules:
  0.0 453.5 jit_solution(2147542960936348266)
XLA Ops:
  2.4 5.3 %collective-permute-start.1 = (f32[2,8,8,1]{3,2,1,0:T(8,128)S(1)}, f32[2,8,8,1]{3,2,1,0:T(8,128)S(1)}, u32[]{:S(2)}, u32[]{:S(2)}) collective-permute-start(f32[2,8,8,1]{3,2,1,0:T(8,128)S(1)} %get-tuple-element.496), channel_id=1, source_target_pairs={{16,0},{32,16},{48,32},{64,48},{80,64},{96,80},{112,96},{128,112},... | collective-permute-start | bytes 1544 | tf_op jit(solution)/shard_map/ppermute | solution.py:52
  8.4 3.0 collective-permute-start.21
  32.1 3.0 collective-permute-start.5
  69.6 3.0 collective-permute-start.9
  104.3 3.0 collective-permute-start.13
  117.5 3.0 collective-permute-done.14
  138.3 3.0 collective-permute-start.17
  142.8 5.3 %collective-permute-start.22 = (f32[1,8,1,130]{3,2,1,0:T(1,128)}, f32[1,8,1,130]{3,2,1,0:T(1,128)}, u32[]{:S(2)}, u32[]{:S(2)}) collective-permute-start(f32[1,8,1,130]{3,2,1,0:T(1,128)} %get-tuple-element.428), channel_id=1, source_target_pairs={{1,0},{2,1},{3,2},{4,3},{5,4},{6,5},{7,6},{8,7},{9,8},{10,9},{11,1... | collective-permute-start | bytes 12488 | tf_op jit(solution)/shard_map/ppermute | solution.py:52
  153.3 5.5 %collective-permute-start.19 = (f32[21,8,1,130]{3,2,1,0:T(1,128)S(1)}, f32[21,8,1,130]{3,2,1,0:T(1,128)S(1)}, u32[]{:S(2)}, u32[]{:S(2)}) collective-permute-start(f32[21,8,1,130]{3,2,1,0:T(1,128)S(1)} %get-tuple-element.328), channel_id=1, source_target_pairs={{1,0},{2,1},{3,2},{4,3},{5,4},{6,5},{7,6},{8,7},{9,8},{10,9},{11,1... | collective-permute-start | bytes 262088 | tf_op jit(solution)/shard_map/ppermute | solution.py:52
  168.0 2.9 collective-permute-start.25
  180.9 5.4 %collective-permute-start.26 = (f32[2,8,1,130]{3,0,2,1:T(2,128)S(1)}, f32[2,8,1,130]{3,0,2,1:T(2,128)S(1)}, u32[]{:S(2)}, u32[]{:S(2)}) collective-permute-start(f32[2,8,1,130]{3,0,2,1:T(2,128)S(1)} %get-tuple-element.402), channel_id=1, source_target_pairs={{1,0},{2,1},{3,2},{4,3},{5,4},{6,5},{7,6},{8,7},{9,8},{10,9},{11,1... | collective-permute-start | bytes 24968 | tf_op jit(solution)/shard_map/ppermute | solution.py:52
  187.7 5.7 %collective-permute-done.27 = f32[2,8,1,130]{3,0,2,1:T(2,128)S(1)} collective-permute-done((f32[2,8,1,130]{3,0,2,1:T(2,128)S(1)}, f32[2,8,1,130]{3,0,2,1:T(2,128)S(1)}, u32[]{:S(2)}, u32[]{:S(2)}) %collective-permute-start.27) | collective-permute-done | bytes 8352 | tf_op jit(solution)/shard_map/ppermute | solution.py:49
  194.2 2.9 collective-permute-start.29
  199.2 5.4 %collective-permute-start.30 = (f32[2,8,1,130]{3,0,2,1:T(2,128)S(1)}, f32[2,8,1,130]{3,0,2,1:T(2,128)S(1)}, u32[]{:S(2)}, u32[]{:S(2)}) collective-permute-start(f32[2,8,1,130]{3,0,2,1:T(2,128)S(1)} %get-tuple-element.398), channel_id=1, source_target_pairs={{1,0},{2,1},{3,2},{4,3},{5,4},{6,5},{7,6},{8,7},{9,8},{10,9},{11,1... | collective-permute-start | bytes 24968 | tf_op jit(solution)/shard_map/ppermute | solution.py:52
  208.9 2.9 collective-permute-start.33
  213.9 3.5 collective-permute-start.34
  226.7 3.5 collective-permute-start.38
  235.5 25.6 %psum.28 = f32[9,9]{1,0:T(8,128)S(1)} all-reduce(f32[9,9]{1,0:T(8,128)S(1)} %convolution_bitcast_fusion.1), channel_id=1, replica_groups=mesh['gx'=16,'gy'=16] {'gx'}, use_global_device_ids=true, to_apply=%region_0.1 | all-reduce | flops 81 | bytes 648 | tf_op jit(solution)/shard_map/psum | solution.py:307
  261.1 39.6 %psum.29 = f32[9,9]{1,0:T(8,128)S(1)} all-reduce(f32[9,9]{1,0:T(8,128)S(1)} %psum.28), channel_id=1, replica_groups=mesh['gx'=16,'gy'=16] {'gy'}, use_global_device_ids=true, to_apply=%region_1.2 | all-reduce | flops 81 | bytes 648 | tf_op jit(solution)/shard_map/psum | solution.py:307
  334.9 5.3 %collective-permute-start.46 = (f32[2,8,1,130]{3,0,2,1:T(2,128)S(1)}, f32[2,8,1,130]{3,0,2,1:T(2,128)S(1)}, u32[]{:S(2)}, u32[]{:S(2)}) collective-permute-start(f32[2,8,1,130]{3,0,2,1:T(2,128)S(1)} %get-tuple-element.392), channel_id=1, source_target_pairs={{1,0},{2,1},{3,2},{4,3},{5,4},{6,5},{7,6},{8,7},{9,8},{10,9},{11,1... | collective-permute-start | bytes 24968 | tf_op jit(solution)/shard_map/ppermute | solution.py:52
  349.5 3.5 collective-permute-start.50
  362.2 3.5 collective-permute-start.54
  371.0 25.6 %psum.30 = f32[9,9]{1,0:T(8,128)S(1)} all-reduce(f32[9,9]{1,0:T(8,128)S(1)} %convolution_bitcast_fusion), channel_id=1, replica_groups=mesh['gx'=16,'gy'=16] {'gx'}, use_global_device_ids=true, to_apply=%region_2.3 | all-reduce | flops 81 | bytes 648 | tf_op jit(solution)/shard_map/psum | solution.py:307
  396.6 39.7 %psum.31 = f32[9,9]{1,0:T(8,128)S(1)} all-reduce(f32[9,9]{1,0:T(8,128)S(1)} %psum.30), channel_id=1, replica_groups=mesh['gx'=16,'gy'=16] {'gy'}, use_global_device_ids=true, to_apply=%region_3.4 | all-reduce | flops 81 | bytes 648 | tf_op jit(solution)/shard_map/psum | solution.py:307
  (950 shorter events, 220.1 us)
Async XLA Ops:
  2.4 9.0 %collective-permute-start = (f32[2,8,8,1]{3,2,1,0:T(8,128)S(1)}, f32[2,8,8,1]{3,2,1,0:T(8,128)S(1)}, u32[]{:S(2)}, u32[]{:S(2)}) collective-permute-start(f32[2,8,8,1]{3,2,1,0:T(8,128)S(1)} %get-tuple-element.495), channel_id=1, source_target_pairs={{0,16},{16,32},{32,48},{48,64},{64,80},{80,96},{96,112},{112,128},... | collective-permute-start | bytes 1544 | tf_op jit(solution)/shard_map/ppermute | solution.py:49
  2.4 9.0 %collective-permute-start.1 = (f32[2,8,8,1]{3,2,1,0:T(8,128)S(1)}, f32[2,8,8,1]{3,2,1,0:T(8,128)S(1)}, u32[]{:S(2)}, u32[]{:S(2)}) collective-permute-start(f32[2,8,8,1]{3,2,1,0:T(8,128)S(1)} %get-tuple-element.496), channel_id=1, source_target_pairs={{16,0},{32,16},{48,32},{64,48},{80,64},{96,80},{112,96},{128,112},... | collective-permute-start | bytes 1544 | tf_op jit(solution)/shard_map/ppermute | solution.py:52
  8.4 132.8 %collective-permute-start.20 = (f32[1,8,8,1]{3,2,1,0:T(8,128)}, f32[1,8,8,1]{3,2,1,0:T(8,128)}, u32[]{:S(2)}, u32[]{:S(2)}) collective-permute-start(f32[1,8,8,1]{3,2,1,0:T(8,128)} %get-tuple-element.508), channel_id=1, source_target_pairs={{0,16},{16,32},{32,48},{48,64},{64,80},{80,96},{96,112},{112,128},... | collective-permute-start | bytes 776 | tf_op jit(solution)/shard_map/ppermute | solution.py:49
  8.4 132.8 %collective-permute-start.21 = (f32[1,8,8,1]{3,2,1,0:T(8,128)}, f32[1,8,8,1]{3,2,1,0:T(8,128)}, u32[]{:S(2)}, u32[]{:S(2)}) collective-permute-start(f32[1,8,8,1]{3,2,1,0:T(8,128)} %get-tuple-element.507), channel_id=1, source_target_pairs={{16,0},{32,16},{48,32},{64,48},{80,64},{96,80},{112,96},{128,112},... | collective-permute-start | bytes 776 | tf_op jit(solution)/shard_map/ppermute | solution.py:52
  31.5 7.9 %collective-permute-start.4 = (f32[21,8,8,1]{0,2,3,1:T(8,128)S(1)}, f32[21,8,8,1]{0,2,3,1:T(8,128)S(1)}, u32[]{:S(2)}, u32[]{:S(2)}) collective-permute-start(f32[21,8,8,1]{0,2,3,1:T(8,128)S(1)} %copy.34), channel_id=1, source_target_pairs={{0,16},{16,32},{32,48},{48,64},{64,80},{80,96},{96,112},{112,128},... | collective-permute-start | bytes 16136 | tf_op jit(solution)/shard_map/ppermute | solution.py:49
  32.1 8.1 %collective-permute-start.5 = (f32[21,8,8,1]{0,2,3,1:T(8,128)S(1)}, f32[21,8,8,1]{0,2,3,1:T(8,128)}, u32[]{:S(2)}, u32[]{:S(2)}) collective-permute-start(f32[21,8,8,1]{0,2,3,1:T(8,128)S(1)} %copy.36), channel_id=1, source_target_pairs={{16,0},{32,16},{48,32},{64,48},{80,64},{96,80},{112,96},{128,112},... | collective-permute-start | bytes 16136 | tf_op jit(solution)/shard_map/ppermute | solution.py:52
  44.3 7.2 %collective-permute-start.7 = (f32[21,8,1,130]{3,2,1,0:T(1,128)S(1)}, f32[21,8,1,130]{3,2,1,0:T(1,128)S(1)}, u32[]{:S(2)}, u32[]{:S(2)}) collective-permute-start(f32[21,8,1,130]{3,2,1,0:T(1,128)S(1)} %get-tuple-element.347), channel_id=1, source_target_pairs={{1,0},{2,1},{3,2},{4,3},{5,4},{6,5},{7,6},{8,7},{9,8},{10,9},{11,1... | collective-permute-start | bytes 262088 | tf_op jit(solution)/shard_map/ppermute | solution.py:52
  69.1 6.6 %collective-permute-start.8 = (f32[21,8,8,1]{0,2,3,1:T(8,128)S(1)}, f32[21,8,8,1]{0,2,3,1:T(8,128)S(1)}, u32[]{:S(2)}, u32[]{:S(2)}) collective-permute-start(f32[21,8,8,1]{0,2,3,1:T(8,128)S(1)} %copy.40), channel_id=1, source_target_pairs={{0,16},{16,32},{32,48},{48,64},{64,80},{80,96},{96,112},{112,128},... | collective-permute-start | bytes 16136 | tf_op jit(solution)/shard_map/ppermute | solution.py:49
  69.6 6.8 %collective-permute-start.9 = (f32[21,8,8,1]{0,2,3,1:T(8,128)S(1)}, f32[21,8,8,1]{0,2,3,1:T(8,128)S(1)}, u32[]{:S(2)}, u32[]{:S(2)}) collective-permute-start(f32[21,8,8,1]{0,2,3,1:T(8,128)S(1)} %copy.42), channel_id=1, source_target_pairs={{16,0},{32,16},{48,32},{64,48},{80,64},{96,80},{112,96},{128,112},... | collective-permute-start | bytes 16136 | tf_op jit(solution)/shard_map/ppermute | solution.py:52
  103.8 6.6 %collective-permute-start.12 = (f32[21,8,8,1]{0,2,3,1:T(8,128)S(1)}, f32[21,8,8,1]{0,2,3,1:T(8,128)S(1)}, u32[]{:S(2)}, u32[]{:S(2)}) collective-permute-start(f32[21,8,8,1]{0,2,3,1:T(8,128)S(1)} %copy.46), channel_id=1, source_target_pairs={{0,16},{16,32},{32,48},{48,64},{64,80},{80,96},{96,112},{112,128},... | collective-permute-start | bytes 16136 | tf_op jit(solution)/shard_map/ppermute | solution.py:49
  104.3 6.8 %collective-permute-start.13 = (f32[21,8,8,1]{0,2,3,1:T(8,128)S(1)}, f32[21,8,8,1]{0,2,3,1:T(8,128)S(1)}, u32[]{:S(2)}, u32[]{:S(2)}) collective-permute-start(f32[21,8,8,1]{0,2,3,1:T(8,128)S(1)} %copy.48), channel_id=1, source_target_pairs={{16,0},{32,16},{48,32},{64,48},{80,64},{96,80},{112,96},{128,112},... | collective-permute-start | bytes 16136 | tf_op jit(solution)/shard_map/ppermute | solution.py:52
  113.2 7.2 %collective-permute-start.14 = (f32[21,8,1,130]{3,2,1,0:T(1,128)S(1)}, f32[21,8,1,130]{3,2,1,0:T(1,128)S(1)}, u32[]{:S(2)}, u32[]{:S(2)}) collective-permute-start(f32[21,8,1,130]{3,2,1,0:T(1,128)S(1)} %get-tuple-element.334), channel_id=1, source_target_pairs={{0,1},{1,2},{2,3},{3,4},{4,5},{5,6},{6,7},{7,8},{8,9},{9,10},{10,1... | collective-permute-start | bytes 262088 | tf_op jit(solution)/shard_map/ppermute | solution.py:49
  137.7 12.6 %collective-permute-start.16 = (f32[21,8,8,1]{0,2,3,1:T(8,128)S(1)}, f32[21,8,8,1]{0,2,3,1:T(8,128)S(1)}, u32[]{:S(2)}, u32[]{:S(2)}) collective-permute-start(f32[21,8,8,1]{0,2,3,1:T(8,128)S(1)} %copy.52), channel_id=1, source_target_pairs={{0,16},{16,32},{32,48},{48,64},{64,80},{80,96},{96,112},{112,128},... | collective-permute-start | bytes 16136 | tf_op jit(solution)/shard_map/ppermute | solution.py:49
  138.3 12.8 %collective-permute-start.17 = (f32[21,8,8,1]{0,2,3,1:T(8,128)S(1)}, f32[21,8,8,1]{0,2,3,1:T(8,128)S(1)}, u32[]{:S(2)}, u32[]{:S(2)}) collective-permute-start(f32[21,8,8,1]{0,2,3,1:T(8,128)S(1)} %copy.54), channel_id=1, source_target_pairs={{16,0},{32,16},{48,32},{64,48},{80,64},{96,80},{112,96},{128,112},... | collective-permute-start | bytes 16136 | tf_op jit(solution)/shard_map/ppermute | solution.py:52
  142.8 23.2 %collective-permute-start.22 = (f32[1,8,1,130]{3,2,1,0:T(1,128)}, f32[1,8,1,130]{3,2,1,0:T(1,128)}, u32[]{:S(2)}, u32[]{:S(2)}) collective-permute-start(f32[1,8,1,130]{3,2,1,0:T(1,128)} %get-tuple-element.428), channel_id=1, source_target_pairs={{1,0},{2,1},{3,2},{4,3},{5,4},{6,5},{7,6},{8,7},{9,8},{10,9},{11,1... | collective-permute-start | bytes 12488 | tf_op jit(solution)/shard_map/ppermute | solution.py:52
  148.2 17.9 %collective-permute-start.23 = (f32[1,8,1,130]{3,2,1,0:T(1,128)}, f32[1,8,1,130]{3,2,1,0:T(1,128)}, u32[]{:S(2)}, u32[]{:S(2)}) collective-permute-start(f32[1,8,1,130]{3,2,1,0:T(1,128)} %get-tuple-element.429), channel_id=1, source_target_pairs={{0,1},{1,2},{2,3},{3,4},{4,5},{5,6},{6,7},{7,8},{8,9},{9,10},{10,1... | collective-permute-start | bytes 12488 | tf_op jit(solution)/shard_map/ppermute | solution.py:49
  153.2 8.9 %collective-permute-start.18 = (f32[21,8,1,130]{3,2,1,0:T(1,128)S(1)}, f32[21,8,1,130]{3,2,1,0:T(1,128)S(1)}, u32[]{:S(2)}, u32[]{:S(2)}) collective-permute-start(f32[21,8,1,130]{3,2,1,0:T(1,128)S(1)} %get-tuple-element.329), channel_id=1, source_target_pairs={{0,1},{1,2},{2,3},{3,4},{4,5},{5,6},{6,7},{7,8},{8,9},{9,10},{10,1... | collective-permute-start | bytes 262088 | tf_op jit(solution)/shard_map/ppermute | solution.py:49
  153.3 8.8 %collective-permute-start.19 = (f32[21,8,1,130]{3,2,1,0:T(1,128)S(1)}, f32[21,8,1,130]{3,2,1,0:T(1,128)S(1)}, u32[]{:S(2)}, u32[]{:S(2)}) collective-permute-start(f32[21,8,1,130]{3,2,1,0:T(1,128)S(1)} %get-tuple-element.328), channel_id=1, source_target_pairs={{1,0},{2,1},{3,2},{4,3},{5,4},{6,5},{7,6},{8,7},{9,8},{10,9},{11,1... | collective-permute-start | bytes 262088 | tf_op jit(solution)/shard_map/ppermute | solution.py:52
  168.0 12.7 %collective-permute-start.24 = (f32[2,8,8,1]{3,0,2,1:T(2,128)S(1)}, f32[2,8,8,1]{3,0,2,1:T(2,128)S(1)}, u32[]{:S(2)}, u32[]{:S(2)}) collective-permute-start(f32[2,8,8,1]{3,0,2,1:T(2,128)S(1)} %get-tuple-element.502), channel_id=1, source_target_pairs={{0,16},{16,32},{32,48},{48,64},{64,80},{80,96},{96,112},{112,128},... | collective-permute-start | bytes 1544 | tf_op jit(solution)/shard_map/ppermute | solution.py:49
  168.0 12.7 %collective-permute-start.25 = (f32[2,8,8,1]{3,0,2,1:T(2,128)S(1)}, f32[2,8,8,1]{3,0,2,1:T(2,128)S(1)}, u32[]{:S(2)}, u32[]{:S(2)}) collective-permute-start(f32[2,8,8,1]{3,0,2,1:T(2,128)S(1)} %get-tuple-element.501), channel_id=1, source_target_pairs={{16,0},{32,16},{48,32},{64,48},{80,64},{96,80},{112,96},{128,112},... | collective-permute-start | bytes 1544 | tf_op jit(solution)/shard_map/ppermute | solution.py:52
  180.9 6.9 %collective-permute-start.26 = (f32[2,8,1,130]{3,0,2,1:T(2,128)S(1)}, f32[2,8,1,130]{3,0,2,1:T(2,128)S(1)}, u32[]{:S(2)}, u32[]{:S(2)}) collective-permute-start(f32[2,8,1,130]{3,0,2,1:T(2,128)S(1)} %get-tuple-element.402), channel_id=1, source_target_pairs={{1,0},{2,1},{3,2},{4,3},{5,4},{6,5},{7,6},{8,7},{9,8},{10,9},{11,1... | collective-permute-start | bytes 24968 | tf_op jit(solution)/shard_map/ppermute | solution.py:52
  186.3 7.1 %collective-permute-start.27 = (f32[2,8,1,130]{3,0,2,1:T(2,128)S(1)}, f32[2,8,1,130]{3,0,2,1:T(2,128)S(1)}, u32[]{:S(2)}, u32[]{:S(2)}) collective-permute-start(f32[2,8,1,130]{3,0,2,1:T(2,128)S(1)} %get-tuple-element.403), channel_id=1, source_target_pairs={{0,1},{1,2},{2,3},{3,4},{4,5},{5,6},{6,7},{7,8},{8,9},{9,10},{10,1... | collective-permute-start | bytes 24968 | tf_op jit(solution)/shard_map/ppermute | solution.py:49
  199.2 6.9 %collective-permute-start.30 = (f32[2,8,1,130]{3,0,2,1:T(2,128)S(1)}, f32[2,8,1,130]{3,0,2,1:T(2,128)S(1)}, u32[]{:S(2)}, u32[]{:S(2)}) collective-permute-start(f32[2,8,1,130]{3,0,2,1:T(2,128)S(1)} %get-tuple-element.398), channel_id=1, source_target_pairs={{1,0},{2,1},{3,2},{4,3},{5,4},{6,5},{7,6},{8,7},{9,8},{10,9},{11,1... | collective-permute-start | bytes 24968 | tf_op jit(solution)/shard_map/ppermute | solution.py:52
  334.9 6.7 %collective-permute-start.46 = (f32[2,8,1,130]{3,0,2,1:T(2,128)S(1)}, f32[2,8,1,130]{3,0,2,1:T(2,128)S(1)}, u32[]{:S(2)}, u32[]{:S(2)}) collective-permute-start(f32[2,8,1,130]{3,0,2,1:T(2,128)S(1)} %get-tuple-element.392), channel_id=1, source_target_pairs={{1,0},{2,1},{3,2},{4,3},{5,4},{6,5},{7,6},{8,7},{9,8},{10,9},{11,1... | collective-permute-start | bytes 24968 | tf_op jit(solution)/shard_map/ppermute | solution.py:52
  (307 other events, 760.3 us)
